TPU v7x, 32 devices: a whole 2x2x4 slice. The times are simulated.
32 devices in a mesh: ctx: 8 (over z, x), head: 4 (over y, core).
Axes of the slice: x: 2, y: 2, z: 4, core: 2. Of those that a mesh axis runs over, the one named last changes fastest.
Arguments:
- query_rows: bfloat16 [1536, 4096], P('ctx', 'head'), may hold values from -4.5 to 4.5
- key_rows: bfloat16 [1536, 512], P('ctx'), may hold values from -4.5 to 4.5
- value_rows: bfloat16 [1536, 512], P('ctx'), may hold values from -6 to 6
- w_out: bfloat16 [4096, 2048], P('head'), may hold values from -0.09375 to 0.09375
Outputs:
- mixed: bfloat16 [1536, 2048], P('ctx', 'head')
All inputs are finite; a program needn't handle non-finite values.
Results may differ from a plain program's by a relative error of at most 0.019.
Values may be sent and summed in bfloat16 or wider, within the bound.
No kernel may reach another device: no remote copies, remote signals or barrier semaphores. Data moves between devices by JAX's collectives and lax.ppermute only.
A program may use at most 64 MiB of HBM per device.

v0:
```python
import math
import jax
import jax.numpy as jnp
from jax import lax
from jax.sharding import PartitionSpec as P

KVH = 4
HD = 128
negative = -1e30


def attend(state, queries_half, position_half, block_keys, block_values, key_start, score_scale):
    maximum, denominator, numerator = state
    key_count = block_keys.shape[0]
    scores = (
        jnp.einsum("thd,kd->thk", queries_half, block_keys, preferred_element_type=jnp.float32)
        * score_scale
    )
    key_positions = key_start + jnp.arange(key_count, dtype=jnp.int32)
    allowed = key_positions[None, None, :] <= position_half[:, None, None]
    scores = jnp.where(allowed, scores, negative)
    updated = jnp.maximum(maximum, jnp.max(scores, axis=2))
    weights = jnp.where(allowed, jnp.exp(scores - updated[:, :, None]), 0.0)
    factor = jnp.exp(maximum - updated)
    denominator = denominator * factor + jnp.sum(weights, axis=2)
    numerator = numerator * factor[:, :, None] + jnp.einsum(
        "thk,kd->thd",
        weights.astype(jnp.bfloat16),
        block_values,
        preferred_element_type=jnp.float32,
    )
    return (updated, denominator, numerator)


def on_device(query_rows, key_rows, value_rows, w_out):
    local_tokens = query_rows.shape[0]
    head_count = lax.axis_size("head")
    local_heads = query_rows.shape[1] // HD
    kv_head = lax.axis_index("head") * KVH // head_count
    own_keys = lax.dynamic_slice_in_dim(key_rows, kv_head * HD, HD, 1)
    own_values = lax.dynamic_slice_in_dim(value_rows, kv_head * HD, HD, 1)
    row_numbers = jnp.arange(local_tokens, dtype=jnp.int32)
    positions = lax.axis_index("ctx") * local_tokens + row_numbers
    heads_view = query_rows.reshape(local_tokens, local_heads, HD)
    half_rows = local_tokens // 2
    halves = [
        (heads_view[:half_rows], positions[:half_rows]),
        (heads_view[half_rows:], positions[half_rows:]),
    ]
    score_scale = 1.0 / math.sqrt(HD)
    initial = (
        jnp.full((half_rows, local_heads), negative, jnp.float32),
        jnp.zeros((half_rows, local_heads), jnp.float32),
        jnp.zeros((half_rows, local_heads, HD), jnp.float32),
    )
    piece_keys = lax.all_gather(own_keys, "ctx", axis=0, tiled=True)
    piece_values = lax.all_gather(own_values, "ctx", axis=0, tiled=True)
    piece_rows = piece_keys.shape[0]
    block_rows = math.gcd(piece_rows, local_tokens * max(1, 1024 // local_tokens))
    block_total = piece_rows // block_rows

    def one_block(block_number, states):
        block_start = block_number * block_rows
        block_keys = lax.dynamic_slice_in_dim(piece_keys, block_start, block_rows, 0)
        block_values = lax.dynamic_slice_in_dim(piece_values, block_start, block_rows, 0)
        results = []
        for (queries_half, position_half), state in zip(halves, states):
            state = attend(
                state,
                queries_half,
                position_half,
                block_keys,
                block_values,
                block_start,
                score_scale,
            )
            results.append(state)
        return tuple(results)

    states = lax.fori_loop(0, block_total, one_block, (initial, initial))
    pieces = [state[2] / state[1][:, :, None] for state in states]
    attended = (
        jnp.concatenate(pieces, axis=0).astype(jnp.bfloat16).reshape(local_tokens, local_heads * HD)
    )
    partial_sums = jnp.dot(attended, w_out, preferred_element_type=jnp.float32)
    return lax.psum_scatter(
        partial_sums.astype(jnp.bfloat16), "head", scatter_dimension=1, tiled=True
    )


def solution(mesh):
    placed = (P("ctx", "head"), P("ctx", None), P("ctx", None), P("head", None))
    return jax.shard_map(
        on_device, mesh=mesh, in_specs=placed, out_specs=P("ctx", "head"), check_vma=False
    )
```

profile of v0, /device:TPU:0, one launch (start us, length us, event | category | flops | bytes accessed | tf_op | source)
XLA Modules:
  0.0 131.6 jit_solution(6765854102075202055)
XLA Ops:
  6.7 0.8 copy-done
  7.5 0.8 constant_dynamic-slice_fusion
  8.3 32.9 %all_gather.7 = bf16[1536,128]{1,0:T(8,128)(2,1)S(1)} all-gather(bf16[192,128]{1,0:T(8,128)(2,1)S(1)} %constant_dynamic-slice_fusion), channel_id=1, replica_groups=mesh['ctx'=8,'head'=4] {'ctx'}, dimensions={0}, use_global_device_ids=true | all-gather | bytes 442368 | tf_op jit(solution)/shard_map/all_gather | solution.py:57
  41.2 30.9 %all_gather.6 = bf16[1536,128]{1,0:T(8,128)(2,1)S(1)} all-gather(bf16[192,128]{1,0:T(8,128)(2,1)S(1)} %constant_dynamic-slice_fusion.1), channel_id=1, replica_groups=mesh['ctx'=8,'head'=4] {'ctx'}, dimensions={0}, use_global_device_ids=true | all-gather | bytes 442368 | tf_op jit(solution)/shard_map/all_gather | solution.py:56
  72.1 1.0 slice_bitcast_fusion
  73.3 22.4 %while.24 = (s32[]{:T(128)}, f32[96,8]{0,1:T(8,128)S(1)}, f32[96,8]{0,1:T(8,128)S(1)}, f32[96,8,128]{2,1,0:T(8,128)S(1)}, f32[96,8]{0,1:T(8,128)S(1)}, /*index=5...) while((s32[]{:T(128)}, f32[96,8]{0,1:T(8,128)S(1)}, ...), condition=%wide.region_5.6_spmd.clone, body=%wide.region_0.5_spmd.clone.sunk | while | flops 153693888 | bytes 7399925 | solution.py:80
  73.4 0.3 fusion.51
  74.0 0.3 copy.33
  74.3 0.3 fusion.52
  74.6 0.2 fusion.53
  75.0 0.3 convolution_add_fusion.4
  75.4 0.3 copy.35
  75.7 0.3 convolution_add_fusion.5
  76.2 0.3 fusion.51
  76.8 0.3 copy.33
  77.1 0.3 fusion.52
  77.5 0.2 fusion.53
  77.8 0.3 convolution_add_fusion.4
  78.2 0.3 copy.35
  78.6 0.3 convolution_add_fusion.5
  79.0 0.3 fusion.51
  79.6 0.3 copy.33
  79.9 0.3 fusion.52
  80.2 0.2 fusion.53
  80.6 0.3 convolution_add_fusion.4
  81.0 0.3 copy.35
  81.3 0.3 convolution_add_fusion.5
  81.8 0.3 fusion.51
  82.4 0.3 copy.33
  82.7 0.3 fusion.52
  83.1 0.2 fusion.53
  83.4 0.3 convolution_add_fusion.4
  83.8 0.3 copy.35
  84.2 0.3 convolution_add_fusion.5
  84.6 0.3 fusion.51
  85.2 0.3 copy.33
  85.5 0.3 fusion.52
  85.8 0.2 fusion.53
  86.2 0.3 convolution_add_fusion.4
  86.6 0.3 copy.35
  86.9 0.3 convolution_add_fusion.5
  87.4 0.3 fusion.51
  88.0 0.3 copy.33
  88.3 0.3 fusion.52
  88.7 0.2 fusion.53
  89.0 0.3 convolution_add_fusion.4
  89.4 0.3 copy.35
  89.8 0.3 convolution_add_fusion.5
  90.2 0.3 fusion.51
  90.8 0.3 copy.33
  91.1 0.3 fusion.52
  91.4 0.2 fusion.53
  91.8 0.3 convolution_add_fusion.4
  92.2 0.3 copy.35
  92.5 0.3 convolution_add_fusion.5
  93.0 0.3 fusion.51
  93.6 0.3 copy.33
  93.9 0.3 fusion.52
  94.3 0.2 fusion.53
  94.6 0.3 convolution_add_fusion.4
  95.0 0.3 copy.35
  95.4 0.3 convolution_add_fusion.5
  96.3 4.1 %convolution_convert_fusion = bf16[192,2048]{1,0:T(8,128)(2,1)} fusion(bf16[1024,2048]{1,0:T(8,128)(2,1)} %param.9, bf16[96,1024]{1,0:T(8,128)(2,1)S(1)} %bitcast.61, bf16[96,1024]{1,0:T(8,128)(2,1)S(1)} %bitcast.62), kind=kOutput, calls=%fused_computation.39 | convolution fusion | flops 806486016 | bytes 5373952 | tf_op jit(solution)/shard_map/dot_general | solution.py:85
  100.4 24.3 %reduce-scatter.2.cloned.1.call-done = bf16[192,512]{1,0:T(8,128)(2,1)} async-done(((bf16[192,2048]{1,0:T(8,128)(2,1)}), bf16[192,512]{1,0:T(8,128)(2,1)}) %reduce-scatter.2.cloned.1.call-update) | async-done | bytes 196624 | tf_op jit(solution)/shard_map/reduce_scatter | solution.py:86
  (99 shorter events, 4.9 us)
Async XLA Ops:
  6.5 0.9 copy-start
  6.5 118.2 %reduce-scatter.2.cloned.1.call-start = ((), (), s32[]{:S(2)}) async-start(), calls=%async_computation.1 | async-start | bytes 983040 | tf_op jit(solution)/shard_map/reduce_scatter | solution.py:86
Sparse Core Ops, SparseCore 0:
  100.5 24.1 reduce-scatter.1
where the time goes:
time: 132 us
  blocking collectives  63.9 us (48%)
  waiting for transfers between devices  24.4 us (18%)
  matrix products  14.4 us (11%)
  between operations  13.5 us (10%)
  local copies, waits for them, and re-layouts  9.8 us (7%)
  other arithmetic  4.6 us (3%)
    all_gather x1, blocking collectives, on_device(): piece_values = lax.all_gather(own_values, 'ctx', axis=0, tiled=True)  32.9 us
    all_gather x1, blocking collectives, on_device(): piece_keys = lax.all_gather(own_keys, 'ctx', axis=0, tiled=True)  30.9 us
    reduce_scatter x1, waiting for transfers between devices, on_device(): lax.psum_scatter(partial_sums.astype(jnp.bfloat16), 'head', scatter_dimen...  24.3 us
    convert_element_type x16, local copies, waits for them, and re-layouts, attend(): weights.astype(jnp.bfloat16)  5.23 us
    dot_general x16, matrix products, attend(): jnp.einsum('thd,kd->thk', queries_half, block_keys, preferred_element_typ...  5.2 us
    dot_general x16, matrix products, attend(): jnp.einsum('thk,kd->thd', weights.astype(jnp.bfloat16), block_values, pre...  5.12 us
    dot_general x1, matrix products, on_device(): partial_sums = jnp.dot(attended, w_out, preferred_element_type=jnp.float32)  4.08 us
    convert_element_type x16, other arithmetic, attend(): weights.astype(jnp.bfloat16)  3.24 us
  transfers between devices with their start and end apart: 1, of which 1 were waited for; matrix products, arithmetic and copies ran while one was open for 0% of the time, Pallas kernels for 0%

commit v1 on v0

--- a/solution.py
+++ b/solution.py
@@ -7,6 +7,28 @@
 KVH = 4
 HD = 128
 negative = -1e30
+
+
+def in_order(blocks, dim):
+    blocks = jnp.moveaxis(blocks, 0, dim)
+    dims = blocks.shape
+    return blocks.reshape(*dims[:dim], dims[dim] * dims[dim + 1], *dims[dim + 2 :])
+
+
+def gather_around(shard, axis, dim):
+    devices = lax.axis_size(axis)
+    pairs = [(i, (i + 1) % devices) for i in range(devices)]
+    back = [(b, a) for a, b in pairs]
+    lower, upper = ([], [])
+    for turn in range(devices - 1):
+        if turn % 2 == 0:
+            lower.append(lax.ppermute(lower[-1] if lower else shard, axis, pairs))
+        else:
+            upper.append(lax.ppermute(upper[-1] if upper else shard, axis, back))
+    blocks = jnp.stack([*lower[::-1], shard, *upper])
+    shift = lax.axis_index(axis) - len(lower)
+    blocks = blocks[(jnp.arange(devices) - shift) % devices]
+    return in_order(blocks, dim)
 
 
 def attend(state, queries_half, position_half, block_keys, block_values, key_start, score_scale):
@@ -54,7 +76,7 @@
         jnp.zeros((half_rows, local_heads, HD), jnp.float32),
     )
     piece_keys = lax.all_gather(own_keys, "ctx", axis=0, tiled=True)
-    piece_values = lax.all_gather(own_values, "ctx", axis=0, tiled=True)
+    piece_values = gather_around(own_values, "ctx", 0)
     piece_rows = piece_keys.shape[0]
     block_rows = math.gcd(piece_rows, local_tokens * max(1, 1024 // local_tokens))
     block_total = piece_rows // block_rows

time: 132 us -> 125 us (0.947)
  blocking collectives: 63.9 us -> 31.4 us
  starting transfers between devices: 0.01 us -> 15.5 us
  waiting for transfers between devices: 24.4 us -> 33.5 us
    all_gather x1 -> x0, blocking collectives: 32.9 us -> none  [on_device(): piece_values = lax.all_gather(own_values, 'ctx', axis=0, tiled=True)]
    ppermute x0 -> x7, starting transfers between devices: none -> 15.5 us  [the longest x3 13.6 us: gather_around(): upper.append(lax.ppermute(upper[-1] if upper else shard, axis, back))]
    ppermute x0 -> x7, waiting for transfers between devices: none -> 9.5 us  [the longest x4 9.49 us: gather_around(): lower.append(lax.ppermute(lower[-1] if lower else shard, axis, pairs))]
  transfers between devices with their start and end apart: 1 -> 8, of which waited for: 1 -> 4; matrix products, arithmetic and copies ran while one was open for 0% -> 2% of each run, Pallas kernels for 0% -> 0%
where the time goes in v1:
time: 125 us
  waiting for transfers between devices  33.5 us (27%)
  blocking collectives  31.4 us (25%)
  starting transfers between devices  15.5 us (12%)
  matrix products  14.4 us (12%)
  between operations  13.6 us (11%)
  local copies, waits for them, and re-layouts  10.6 us (8%)
  other arithmetic  4.63 us (4%)
    all_gather x1, blocking collectives, on_device(): piece_keys = lax.all_gather(own_keys, 'ctx', axis=0, tiled=True)  31.4 us
    reduce_scatter x1, waiting for transfers between devices, on_device(): lax.psum_scatter(partial_sums.astype(jnp.bfloat16), 'head', scatter_dimen...  24 us
    ppermute x3, starting transfers between devices, gather_around(): upper.append(lax.ppermute(upper[-1] if upper else shard, axis, back))  13.6 us
    ppermute x4, waiting for transfers between devices, gather_around(): lower.append(lax.ppermute(lower[-1] if lower else shard, axis, pairs))  9.49 us
    convert_element_type x16, local copies, waits for them, and re-layouts, attend(): weights.astype(jnp.bfloat16)  5.27 us
    dot_general x16, matrix products, attend(): jnp.einsum('thd,kd->thk', queries_half, block_keys, preferred_element_typ...  5.2 us
    dot_general x16, matrix products, attend(): jnp.einsum('thk,kd->thd', weights.astype(jnp.bfloat16), block_values, pre...  5.15 us
    dot_general x1, matrix products, on_device(): partial_sums = jnp.dot(attended, w_out, preferred_element_type=jnp.float32)  4.09 us
  transfers between devices with their start and end apart: 8, of which 4 were waited for; matrix products, arithmetic and copies ran while one was open for 2% of the time, Pallas kernels for 0%

profile of v1, /device:TPU:0, one launch (start us, length us, event | category | flops | bytes accessed | tf_op | source)
XLA Modules:
  0.0 124.7 jit_solution(14989432439113545639)
XLA Ops:
  6.5 0.8 constant_dynamic-slice_fusion
  7.4 6.0 %collective-permute-start.4 = (bf16[192,128]{1,0:T(8,128)(2,1)S(1)}, bf16[192,128]{1,0:T(8,128)(2,1)S(1)}, u32[]{:S(2)}, u32[]{:S(2)}) collective-permute-start(bf16[192,128]{1,0:T(8,128)(2,1)S(1)} %constant_dynamic-slice_fusion), channel_id=1, source_target_pairs={{4,0},{8,4},{12,8},{16,12},{20,16},{24,20},{28,24},{0,28},{5,1},{9... | collective-permute-start | bytes 147464 | tf_op jit(solution)/shard_map/ppermute | solution.py:27
  13.5 1.0 slice_bitcast_fusion
  14.6 5.5 %collective-permute-done = bf16[192,128]{1,0:T(8,128)(2,1)S(1)} collective-permute-done((bf16[192,128]{1,0:T(8,128)(2,1)S(1)}, bf16[192,128]{1,0:T(8,128)(2,1)S(1)}, u32[]{:S(2)}, u32[]{:S(2)}) %collective-permute-start) | collective-permute-done | bytes 49184 | tf_op jit(solution)/shard_map/ppermute | solution.py:25
  20.2 31.4 %all_gather.3 = bf16[1536,128]{1,0:T(8,128)(2,1)S(1)} all-gather(bf16[192,128]{1,0:T(8,128)(2,1)S(1)} %constant_dynamic-slice_fusion.1), channel_id=1, replica_groups=mesh['ctx'=8,'head'=4] {'ctx'}, dimensions={0}, use_global_device_ids=true | all-gather | bytes 442368 | tf_op jit(solution)/shard_map/all_gather | solution.py:78
  51.6 1.9 %collective-permute-start.2 = (bf16[192,128]{1,0:T(8,128)(2,1)S(1)}, bf16[192,128]{1,0:T(8,128)(2,1)S(1)}, u32[]{:S(2)}, u32[]{:S(2)}) collective-permute-start(bf16[192,128]{1,0:T(8,128)(2,1)S(1)} %collective-permute-done.1), channel_id=1, source_target_pairs={{0,4},{4,8},{8,12},{12,16},{16,20},{20,24},{24,28},{28,0},{1,5},{5... | collective-permute-start | bytes 147464 | tf_op jit(solution)/shard_map/ppermute | solution.py:25
  53.5 2.8 %collective-permute-start.5 = (bf16[192,128]{1,0:T(8,128)(2,1)S(1)}, bf16[192,128]{1,0:T(8,128)(2,1)S(1)}, u32[]{:S(2)}, u32[]{:S(2)}) collective-permute-start(bf16[192,128]{1,0:T(8,128)(2,1)S(1)} %collective-permute-done.4), channel_id=1, source_target_pairs={{4,0},{8,4},{12,8},{16,12},{20,16},{24,20},{28,24},{0,28},{5,1},{9... | collective-permute-start | bytes 147464 | tf_op jit(solution)/shard_map/ppermute | solution.py:27
  56.4 2.0 %collective-permute-done.2 = bf16[192,128]{1,0:T(8,128)(2,1)S(1)} collective-permute-done((bf16[192,128]{1,0:T(8,128)(2,1)S(1)}, bf16[192,128]{1,0:T(8,128)(2,1)S(1)}, u32[]{:S(2)}, u32[]{:S(2)}) %collective-permute-start.2) | collective-permute-done | bytes 49184 | tf_op jit(solution)/shard_map/ppermute | solution.py:25
  58.4 4.7 %collective-permute-start.6 = (bf16[192,128]{1,0:T(8,128)(2,1)S(1)}, bf16[192,128]{1,0:T(8,128)(2,1)S(1)}, u32[]{:S(2)}, u32[]{:S(2)}) collective-permute-start(bf16[192,128]{1,0:T(8,128)(2,1)S(1)} %collective-permute-done.5), channel_id=1, source_target_pairs={{4,0},{8,4},{12,8},{16,12},{20,16},{24,20},{28,24},{0,28},{5,1},{9... | collective-permute-start | bytes 147464 | tf_op jit(solution)/shard_map/ppermute | solution.py:27
  63.2 2.0 %collective-permute-done.3 = bf16[192,128]{1,0:T(8,128)(2,1)S(1)} collective-permute-done((bf16[192,128]{1,0:T(8,128)(2,1)S(1)}, bf16[192,128]{1,0:T(8,128)(2,1)S(1)}, u32[]{:S(2)}, u32[]{:S(2)}) %collective-permute-start.3) | collective-permute-done | bytes 49184 | tf_op jit(solution)/shard_map/ppermute | solution.py:25
  65.2 0.8 bitcast_dynamic-update-slice_fusion.3
  66.1 0.6 gather_fusion
  66.7 22.4 %while.24 = (s32[]{:T(128)}, f32[96,8]{0,1:T(8,128)S(1)}, f32[96,8]{0,1:T(8,128)S(1)}, f32[96,8,128]{2,1,0:T(8,128)S(1)}, f32[96,8]{0,1:T(8,128)S(1)}, /*index=5...) while((s32[]{:T(128)}, f32[96,8]{0,1:T(8,128)S(1)}, ...), condition=%wide.region_5.6_spmd.clone, body=%wide.region_0.5_spmd.clone.sunk | while | flops 153693888 | bytes 7399925 | solution.py:102
  66.8 0.3 fusion.53
  67.4 0.3 copy.33
  67.7 0.3 fusion.54
  68.1 0.2 fusion.55
  68.4 0.3 convolution_add_fusion.4
  68.8 0.3 copy.35
  69.2 0.3 convolution_add_fusion.5
  69.6 0.3 fusion.53
  70.2 0.3 copy.33
  70.5 0.3 fusion.54
  71.2 0.3 convolution_add_fusion.4
  71.6 0.3 copy.35
  72.0 0.3 convolution_add_fusion.5
  72.4 0.3 fusion.53
  73.0 0.3 copy.33
  73.3 0.3 fusion.54
  74.0 0.3 convolution_add_fusion.4
  74.4 0.3 copy.35
  74.8 0.3 convolution_add_fusion.5
  75.2 0.3 fusion.53
  75.8 0.3 copy.33
  76.1 0.3 fusion.54
  76.8 0.3 convolution_add_fusion.4
  77.2 0.3 copy.35
  77.6 0.3 convolution_add_fusion.5
  78.0 0.3 fusion.53
  78.6 0.3 copy.33
  78.9 0.3 fusion.54
  79.6 0.3 convolution_add_fusion.4
  80.0 0.3 copy.35
  80.4 0.3 convolution_add_fusion.5
  80.8 0.3 fusion.53
  81.4 0.3 copy.33
  81.7 0.3 fusion.54
  82.4 0.3 convolution_add_fusion.4
  82.8 0.3 copy.35
  83.2 0.3 convolution_add_fusion.5
  83.6 0.3 fusion.53
  84.2 0.3 copy.33
  84.5 0.3 fusion.54
  85.2 0.3 convolution_add_fusion.4
  85.6 0.3 copy.35
  86.0 0.3 convolution_add_fusion.5
  86.5 0.3 fusion.53
  87.0 0.3 copy.33
  87.3 0.3 fusion.54
  88.0 0.3 convolution_add_fusion.4
  88.5 0.3 copy.35
  88.8 0.3 convolution_add_fusion.5
  89.7 4.1 %convolution_convert_fusion = bf16[192,2048]{1,0:T(8,128)(2,1)} fusion(bf16[1024,2048]{1,0:T(8,128)(2,1)} %param.9, bf16[96,1024]{1,0:T(8,128)(2,1)S(1)} %bitcast.81, bf16[96,1024]{1,0:T(8,128)(2,1)S(1)} %bitcast.82), kind=kOutput, calls=%fused_computation.40 | convolution fusion | flops 806486016 | bytes 5373952 | tf_op jit(solution)/shard_map/dot_general | solution.py:107
  93.9 24.0 %reduce-scatter.2.cloned.1.call-done = bf16[192,512]{1,0:T(8,128)(2,1)} async-done(((bf16[192,2048]{1,0:T(8,128)(2,1)}), bf16[192,512]{1,0:T(8,128)(2,1)}) %reduce-scatter.2.cloned.1.call-update) | async-done | bytes 196624 | tf_op jit(solution)/shard_map/reduce_scatter | solution.py:108
  (123 shorter events, 6.5 us)
Async XLA Ops:
  6.5 8.1 %copy-start = (bf16[192,512]{1,0:T(8,128)(2,1)S(1)}, bf16[192,512]{1,0:T(8,128)(2,1)}, u32[]{:S(2)}) copy-start(bf16[192,512]{1,0:T(8,128)(2,1)} %param.7) | copy-start | bytes 589828
  6.5 111.3 %reduce-scatter.2.cloned.1.call-start = ((), (), s32[]{:S(2)}) async-start(), calls=%async_computation.1 | async-start | bytes 983040 | tf_op jit(solution)/shard_map/reduce_scatter | solution.py:108
  7.4 46.1 %collective-permute-start.4 = (bf16[192,128]{1,0:T(8,128)(2,1)S(1)}, bf16[192,128]{1,0:T(8,128)(2,1)S(1)}, u32[]{:S(2)}, u32[]{:S(2)}) collective-permute-start(bf16[192,128]{1,0:T(8,128)(2,1)S(1)} %constant_dynamic-slice_fusion), channel_id=1, source_target_pairs={{4,0},{8,4},{12,8},{16,12},{20,16},{24,20},{28,24},{0,28},{5,1},{9... | collective-permute-start | bytes 147464 | tf_op jit(solution)/shard_map/ppermute | solution.py:27
  13.4 6.8 %collective-permute-start = (bf16[192,128]{1,0:T(8,128)(2,1)S(1)}, bf16[192,128]{1,0:T(8,128)(2,1)S(1)}, u32[]{:S(2)}, u32[]{:S(2)}) collective-permute-start(bf16[192,128]{1,0:T(8,128)(2,1)S(1)} %constant_dynamic-slice_fusion), channel_id=1, source_target_pairs={{0,4},{4,8},{8,12},{12,16},{16,20},{20,24},{24,28},{28,0},{1,5},{5... | collective-permute-start | bytes 147464 | tf_op jit(solution)/shard_map/ppermute | solution.py:25
  20.2 31.4 %collective-permute-start.1 = (bf16[192,128]{1,0:T(8,128)(2,1)S(1)}, bf16[192,128]{1,0:T(8,128)(2,1)S(1)}, u32[]{:S(2)}, u32[]{:S(2)}) collective-permute-start(bf16[192,128]{1,0:T(8,128)(2,1)S(1)} %collective-permute-done), channel_id=1, source_target_pairs={{0,4},{4,8},{8,12},{12,16},{16,20},{20,24},{24,28},{28,0},{1,5},{5... | collective-permute-start | bytes 147464 | tf_op jit(solution)/shard_map/ppermute | solution.py:25
  51.6 6.8 %collective-permute-start.2 = (bf16[192,128]{1,0:T(8,128)(2,1)S(1)}, bf16[192,128]{1,0:T(8,128)(2,1)S(1)}, u32[]{:S(2)}, u32[]{:S(2)}) collective-permute-start(bf16[192,128]{1,0:T(8,128)(2,1)S(1)} %collective-permute-done.1), channel_id=1, source_target_pairs={{0,4},{4,8},{8,12},{12,16},{16,20},{20,24},{24,28},{28,0},{1,5},{5... | collective-permute-start | bytes 147464 | tf_op jit(solution)/shard_map/ppermute | solution.py:25
  53.5 4.9 %collective-permute-start.5 = (bf16[192,128]{1,0:T(8,128)(2,1)S(1)}, bf16[192,128]{1,0:T(8,128)(2,1)S(1)}, u32[]{:S(2)}, u32[]{:S(2)}) collective-permute-start(bf16[192,128]{1,0:T(8,128)(2,1)S(1)} %collective-permute-done.4), channel_id=1, source_target_pairs={{4,0},{8,4},{12,8},{16,12},{20,16},{24,20},{28,24},{0,28},{5,1},{9... | collective-permute-start | bytes 147464 | tf_op jit(solution)/shard_map/ppermute | solution.py:27
  58.3 6.8 %collective-permute-start.3 = (bf16[192,128]{1,0:T(8,128)(2,1)S(1)}, bf16[192,128]{1,0:T(8,128)(2,1)S(1)}, u32[]{:S(2)}, u32[]{:S(2)}) collective-permute-start(bf16[192,128]{1,0:T(8,128)(2,1)S(1)} %collective-permute-done.2), channel_id=1, source_target_pairs={{0,4},{4,8},{8,12},{12,16},{16,20},{20,24},{24,28},{28,0},{1,5},{5... | collective-permute-start | bytes 147464 | tf_op jit(solution)/shard_map/ppermute | solution.py:25
  58.4 7.6 %collective-permute-start.6 = (bf16[192,128]{1,0:T(8,128)(2,1)S(1)}, bf16[192,128]{1,0:T(8,128)(2,1)S(1)}, u32[]{:S(2)}, u32[]{:S(2)}) collective-permute-start(bf16[192,128]{1,0:T(8,128)(2,1)S(1)} %collective-permute-done.5), channel_id=1, source_target_pairs={{4,0},{8,4},{12,8},{16,12},{20,16},{24,20},{28,24},{0,28},{5,1},{9... | collective-permute-start | bytes 147464 | tf_op jit(solution)/shard_map/ppermute | solution.py:27
Sparse Core Ops, SparseCore 0:
  94.0 23.8 reduce-scatter.1
